TPU v7x, 32 devices: a whole 2x2x4 slice. The times are simulated.
32 devices in a mesh: context: 16 (over z, x, core), tensor: 2 (over y).
Axes of the slice: x: 2, y: 2, z: 4, core: 2. Of those that a mesh axis runs over, the one named last changes fastest.
Arguments:
- head_inputs: bfloat16 [2048, 8192], P('context', 'tensor'), may hold values from -6 to 6
- step_sizes: float32 [128, 2048], P('tensor', 'context'), may hold values from 0.5 to 1.5
- decay_rate: float32 [128], P('tensor'), may hold values from 0.000146484375 to 0.05
- input_map: bfloat16 [2048, 1024], P('context', 'tensor'), may hold values from -0.5 to 0.5
- output_map: bfloat16 [2048, 1024], P('context', 'tensor'), may hold values from -0.5 to 0.5
- document: int32 [2048], P('context'), may hold values from 0 to 2, never falling along the last dimension, each value on 1 to 1024 neighbouring positions
- grad_output: bfloat16 [2048, 8192], P(('context', 'tensor')), may hold values from -6 to 6
Outputs:
- grad_inputs: bfloat16 [2048, 8192], P('context', 'tensor')
- grad_steps: float32 [128, 2048], P('tensor', 'context')
- grad_in_map: float32 [2048, 1024], P('context', 'tensor')
- grad_out_map: float32 [2048, 1024], P('context', 'tensor')
Inputs may be any that keep to these rules, and one draw needn't show every extreme that they name: document numbers never fall along the tokens; each document has 1 to 1024 tokens, one exactly 1024.
All inputs are finite; a program needn't handle non-finite values.
Results may differ from a plain program's by a relative error of at most 0.001.
Values may be sent and summed in bfloat16 or wider, within the bound.
A program may use at most 192 MiB of HBM per device.

v0:
```python
import jax
import jax.numpy as jnp
from jax import lax
from jax.sharding import PartitionSpec as P

H = 128
P_SIZE = 64
N = 128
G = 8
BLOCK = 128
HIGH = lax.Precision.HIGHEST


def padded(cells, sides, width):
    for axis, dim in sides:
        count = lax.axis_size(axis)
        ends = count - 1
        head = lax.slice_in_dim(cells, 0, width, axis=dim)
        tail = lax.slice_in_dim(cells, cells.shape[dim] - width, cells.shape[dim], axis=dim)
        cells = jnp.concatenate(
            [
                lax.ppermute(tail, axis, [(i, (i + 1) % count) for i in range(ends)]),
                cells,
                lax.ppermute(head, axis, [((i + 1) % count, i) for i in range(ends)]),
            ],
            axis=dim,
        )
    return cells


def entering(part, axis, combine, identity, reverse):
    count = lax.axis_size(axis)
    place = lax.axis_index(axis)
    ahead = count - 1 - place if reverse else place
    gathered = jax.tree.map(lambda a: lax.all_gather(a, axis), part)
    state = jax.tree.map(lambda a, e: jnp.zeros_like(a) + jnp.asarray(e, a.dtype), part, identity)

    def one(step, state):
        source = count - 1 - step if reverse else step
        return combine(
            state, jax.tree.map(lambda a: lax.dynamic_index_in_dim(a, source, 0, False), gathered)
        )

    return lax.fori_loop(0, ahead, one, state)


def link_pairs(earlier, later):
    decay_late = later[0]
    spread = decay_late.reshape(decay_late.shape + (1,) * (earlier[1].ndim - decay_late.ndim))
    return (earlier[0] * decay_late, spread * earlier[1] + later[1])


def shards(head_inputs, step_sizes, decay_rate, input_map, output_map, document, grad_output):
    heads_here = decay_rate.shape[0]
    tokens_here = head_inputs.shape[0]
    per_group = H // G
    groups_here = heads_here // per_group
    span = min(BLOCK, tokens_here)
    count = tokens_here // span
    local_grads = lax.all_to_all(grad_output, "tensor", split_axis=1, concat_axis=0, tiled=True)
    shifted_ids = document + 1
    rim = padded(shifted_ids, (("context", 0),), 1)
    prev_id = rim[0] - 1
    next_id = rim[-1] - 1
    ids_blocks = document.reshape(count, span)
    prev_blocks = jnp.concatenate([prev_id[None], ids_blocks[:-1, -1]])
    next_blocks = jnp.concatenate([ids_blocks[1:, 0], next_id[None]])
    positions = jnp.arange(span)
    lower = positions[:, None] >= positions[None, :]
    mask_blocks = (ids_blocks[:, :, None] == ids_blocks[:, None, :]) & lower[None]
    steps_heads = step_sizes.reshape(groups_here, per_group, count, span)
    rates = decay_rate.reshape(groups_here, per_group)
    cumul = jnp.cumsum(-rates[:, :, None, None] * steps_heads, axis=-1)
    step_rows = jnp.transpose(step_sizes).reshape(count, span, groups_here, per_group)
    inputs_f = head_inputs.astype(jnp.float32).reshape(count, span, groups_here, per_group, P_SIZE)
    scaled = inputs_f * step_rows[..., None]
    grads_f = local_grads.astype(jnp.float32).reshape(count, span, groups_here, per_group, P_SIZE)
    in_bf = input_map.reshape(count, span, groups_here, N)
    out_bf = output_map.reshape(count, span, groups_here, N)
    in_f = in_bf.astype(jnp.float32)
    out_f = out_bf.astype(jnp.float32)
    differ = cumul[..., :, None] - cumul[..., None, :]
    weights = jnp.where(
        mask_blocks[None, None], jnp.exp(jnp.where(mask_blocks[None, None], differ, 0.0)), 0.0
    )
    last_sum = cumul[..., -1:]
    in_coef = jnp.exp(cumul) * (ids_blocks == prev_blocks[:, None]).astype(jnp.float32)
    out_coef = jnp.exp(last_sum - cumul) * (ids_blocks == next_blocks[:, None]).astype(jnp.float32)
    end_coef = jnp.exp(last_sum - cumul) * (ids_blocks == ids_blocks[:, -1:]).astype(jnp.float32)
    block_link = (ids_blocks[:, -1] == prev_blocks).astype(jnp.float32)
    block_decay = jnp.exp(last_sum[..., 0]) * block_link
    fresh = jnp.einsum("kjgn,ghkj,kjghp->kghnp", in_f, end_coef, scaled, precision=HIGH)
    message = jnp.einsum("kign,ghki,kighp->kghnp", out_f, in_coef, grads_f, precision=HIGH)
    running = jnp.zeros_like(fresh[0])
    running_decay = jnp.ones_like(block_decay[..., 0])
    index = 0
    inner_states = running
    inner_decays = running_decay
    running = block_decay[..., index, None, None] * running + fresh[index]
    running_decay = block_decay[..., index] * running_decay
    later_states = [None] * count
    later_decays = [None] * count
    behind = jnp.zeros_like(message[0])
    behind_decay = jnp.ones_like(block_decay[..., 0])
    index = 0
    later_states[index] = behind
    later_decays[index] = behind_decay
    behind = block_decay[..., index, None, None] * behind + message[index]
    behind_decay = block_decay[..., index] * behind_decay
    _, incoming = entering(
        (running_decay, running),
        "context",
        link_pairs,
        (jnp.ones_like(running_decay), jnp.zeros_like(running)),
        False,
    )
    _, adjoint = entering(
        (behind_decay, behind),
        "context",
        link_pairs,
        (jnp.ones_like(behind_decay), jnp.zeros_like(behind)),
        True,
    )
    entry_states = jnp.stack([inner_decays[..., None, None] * incoming + inner_states], axis=0)
    exit_adjoints = jnp.stack(
        [later_decays[0][..., None, None] * adjoint + later_states[0]], axis=0
    )
    cross = jnp.einsum("kign,kjgn->gkij", out_bf, in_bf, preferred_element_type=jnp.float32)
    mixing = weights * cross[:, None]
    state_rows = jnp.einsum("kign,kghnp,ghki->kighp", out_f, entry_states, in_coef, precision=HIGH)
    adjoint_rows = jnp.einsum(
        "kjgn,kghnp,ghkj->kjghp", in_f, exit_adjoints, out_coef, precision=HIGH
    )
    carried_c = jnp.einsum("kighp,kghnp,ghki->kign", grads_f, entry_states, in_coef, precision=HIGH)
    carried_b = jnp.einsum(
        "kjghp,kghnp,ghkj->kjgn", scaled, exit_adjoints, out_coef, precision=HIGH
    )
    outputs = jnp.einsum("ghkij,kjghp->kighp", mixing, scaled, precision=HIGH) + state_rows
    update = jnp.einsum("ghkij,kighp->kjghp", mixing, grads_f, precision=HIGH) + adjoint_rows
    slope_rows = jnp.sum(grads_f * outputs, axis=-1) - jnp.sum(scaled * update, axis=-1)
    step_rows_part = jnp.sum(inputs_f * update, axis=-1)
    grad_inputs = (
        (update * step_rows[..., None])
        .reshape(tokens_here, heads_here * P_SIZE)
        .astype(jnp.bfloat16)
    )
    products = jnp.einsum("kighp,kjghp->ghkij", grads_f, scaled, precision=HIGH)
    score_grad = jnp.sum(weights * products, axis=1)
    grad_out_map = (
        jnp.einsum("gkij,kjgn->kign", score_grad, in_f, precision=HIGH) + carried_c
    ).reshape(tokens_here, groups_here * N)
    grad_in_map = (
        jnp.einsum("gkij,kign->kjgn", score_grad, out_f, precision=HIGH) + carried_b
    ).reshape(tokens_here, groups_here * N)
    slopes = jnp.transpose(slope_rows, (2, 3, 0, 1)).reshape(heads_here, tokens_here)
    step_terms = jnp.transpose(step_rows_part, (2, 3, 0, 1)).reshape(heads_here, tokens_here)
    token_index = jnp.arange(tokens_here)
    same_doc = (document[:, None] == document[None, :]) & (
        token_index[:, None] >= token_index[None, :]
    )
    tails_local = jnp.dot(
        slopes, same_doc.astype(jnp.float32), precision=HIGH, preferred_element_type=jnp.float32
    )
    tail_message = jnp.sum(slopes * (document == prev_id).astype(jnp.float32)[None, :], axis=1)
    linked = (document[-1] == prev_id).astype(jnp.float32)
    tail_link = linked * jnp.ones((heads_here,), jnp.float32)
    _, tail_carry = entering(
        (tail_link, tail_message),
        "context",
        link_pairs,
        (jnp.ones_like(tail_link), jnp.zeros_like(tail_message)),
        True,
    )
    tails = tails_local + tail_carry[:, None] * (document == next_id).astype(jnp.float32)[None, :]
    grad_steps = step_terms - decay_rate[:, None] * tails
    return (grad_inputs, grad_steps, grad_in_map, grad_out_map)


def solution(mesh):
    placed = (
        P("context", "tensor"),
        P("tensor", "context"),
        P("tensor"),
        P("context", "tensor"),
        P("context", "tensor"),
        P("context"),
        P(("context", "tensor"), None),
    )
    return jax.shard_map(
        shards,
        mesh=mesh,
        in_specs=placed,
        out_specs=(
            P("context", "tensor"),
            P("tensor", "context"),
            P("context", "tensor"),
            P("context", "tensor"),
        ),
        check_vma=False,
    )
```

profile of v0, /device:TPU:0, one launch (start us, length us, event | category | flops | bytes accessed | tf_op | source)
XLA Modules:
  0.0 581.5 jit_solution(4755453482523883967)
XLA Ops:
  8.5 2.9 collective-permute-start.1
  27.4 3.6 all-to-all-start
  32.0 12.9 %all-to-all-done = bf16[64,2,4096]{2,0,1:T(8,128)(2,1)S(1)} async-done(((bf16[64,2,4096]{2,0,1:T(8,128)(2,1)}), bf16[64,2,4096]{2,0,1:T(8,128)(2,1)S(1)}, u32[]{:S(2)}, u32[]{:S(2)}) %all-to-all-start) | async-done | bytes 1048608 | tf_op jit(solution)/shard_map/all_to_all | solution.py:60
  44.9 3.3 reshape.364
  48.2 4.0 copy.98
  52.2 3.8 fusion.14
  60.3 6.9 %fusion.2 = f32[4,16,64,128]{3,2,1,0:T(8,128)} fusion(f32[4,128,128]{1,2,0:T(8,128)S(1)} %fusion.62, f32[4,16,128]{2,1,0:T(8,128)} %bitcast.206, pred[128,128]{0,1:T(8,128)(4,1)S(1)} %fusion.55, f32[128,4,16,64]{0,3,2,1:T(8,128)S(1)} %bitcast.183, f32[128,4,16]{0,2,1:T(8,128)} %bitcast.198), kind=kOutput, calls=%fused_computation.12 | convolution fusion | flops 810024960 | bytes 4538368 | tf_op jit(solution)/shard_map/ghkij,kjghp->kighp/dot_general | solution.py:138
  70.3 35.9 %all-reduce = f32[16]{0:T(128)} all-reduce(f32[16]{0:T(128)} %dynamic-update-slice), channel_id=2, replica_groups=mesh['context'=16,'tensor'=2] {'context'}, use_global_device_ids=true, to_apply=%add | all-reduce | flops 16 | bytes 128
  106.2 19.4 %all-gather = f32[64,16,1,1]{1,3,2,0:T(1,128)} all-gather(f32[4,16,1,1]{1,3,2,0:T(1,128)} %bitcast.214), channel_id=3, replica_groups=mesh['context'=16,'tensor'=2] {'context'}, dimensions={0}, use_global_device_ids=true | all-gather | bytes 4352 | tf_op jit(solution)/shard_map/all_gather | solution.py:35
  127.2 4.6 reshape.373
  131.8 4.9 copy.112
  136.7 5.7 fusion
  144.5 6.2 %fusion.4 = f32[4,16,128,64]{2,3,1,0:T(8,128)} fusion(bf16[128,4,16,64]{0,3,2,1:T(8,128)(2,1)S(1)} %copy-done.2, f32[4,128,128]{1,2,0:T(8,128)S(1)} %copy-done.13, f32[4,16,128]{2,1,0:T(8,128)S(1)} %bitcast.208, pred[128,128]{0,1:T(8,128)(4,1)S(1)} %fusion.55), kind=kOutput, calls=%fused_computation.13 | convolution fusion | flops 809500672 | bytes 3457024 | tf_op jit(solution)/shard_map/ghkij,kighp->kjghp/dot_general | solution.py:139
  150.7 47.4 %all-gather.7.cloned.1.call-done = f32[16,4,16,128,64]{3,4,2,1,0:T(8,128)} async-done(((f32[1,4,16,128,64]{3,4,2,1,0:T(8,128)}), f32[16,4,16,128,64]{3,4,2,1,0:T(8,128)}) %all-gather.7.cloned.1.call-update) | async-done | bytes 33554448 | tf_op jit(solution)/shard_map/all_gather | solution.py:35
  201.3 6.8 %fusion.38 = f32[1,128,4,128]{1,3,2,0:T(8,128)} fusion(f32[1,128,4,128]{1,3,2,0:T(8,128)} %convolution_bitcast_fusion, f32[4,16,128,64]{3,2,1,0:T(8,128)} %get-tuple-element.217, bf16[128,4,16,64]{0,3,2,1:T(8,128)(2,1)S(1)} %copy-done.2, f32[4,16,128]{2,1,0:T(8,128)S(1)} %copy-done.9), kind=kOutput, calls=%fused_computation.55 | convolution fusion | flops 806420480 | bytes 3702784 | tf_op jit(solution)/shard_map/kighp,kghnp,ghki->kign/dot_general | solution.py:134
  210.0 6.9 %fusion.11 = f32[128,4,16]{0,2,1:T(8,128)} fusion(f32[1,128,4,16,64]{1,4,3,2,0:T(8,128)S(1)} %copy-done.3, f32[4,16,64,128]{3,2,1,0:T(8,128)} %fusion.2, f32[4,16,128,64]{3,2,1,0:T(8,128)} %get-tuple-element.217, f32[128,4,16]{0,2,1:T(8,128)S(1)} %bitcast.204, bf16[128,4,128,1]{2,1,0,3:T(4,128)(2,1)S(1)} %bitcast.193), kind=kOutput, calls=%fused_computation.21 | convolution fusion | flops 807395328 | bytes 6488064 | tf_op jit(solution)/shard_map/kign,kghnp,ghki->kighp/dot_general | solution.py:130
  216.9 151.2 %all-gather.5.cloned.1.call-done = f32[16,4,16,128,64]{3,4,2,1,0:T(8,128)} async-done(((f32[1,4,16,128,64]{3,4,2,1,0:T(8,128)}), f32[16,4,16,128,64]{3,4,2,1,0:T(8,128)}) %all-gather.5.cloned.1.call-update) | async-done | bytes 33554448 | tf_op jit(solution)/shard_map/all_gather | solution.py:35
  370.7 167.5 %while.40 = (s32[]{:T(128)}, f32[4,16,128,64]{3,2,1,0:T(8,128)}, s32[]{:T(128)}, f32[16,4,16]{2,1,0:T(4,128)}, f32[16,4,16,128,64]{3,4,2,1,0:T(8,128)}, /*index=5*/s32[]{:T(128)}, s32[]{:T(128)}, s32[]{:T(128)}, s32[]{:T(128)}) while((s32[]{:T(128)}, f32[4,16,128,64]{3,2,1,0:T(8,128)}, s32[]{:T(128)}, f32[16,4,16]{2,1,0:T(4,128)}, ...), condition=%wide.region_2.3_spmd, body=%wide.region_1.2_spmd.sunk | while | flops 1048582 | bytes 14680979 | solution.py:44
  372.5 2.8 copy.164
  375.9 6.0 %bitcast_add_fusion.10 = f32[4,16,128,64]{3,2,1,0:T(8,128)} fusion(f32[1,4,16,128,64]{4,3,2,1,0:T(8,128)} %copy.164, f32[4,16,128,64]{3,2,1,0:T(8,128)} %get-tuple-element.426, f32[4,16]{1,0:T(4,128)S(1)} %dynamic-slice_bitcast_fusion.4), kind=kLoop, calls=%fused_computation.clone.1 | loop fusion | flops 1048576 | bytes 6291712 | tf_op jit(solution)/shard_map/while/body/add | solution.py:50
  387.0 6.0 %bitcast_add_fusion.10 = f32[4,16,128,64]{3,2,1,0:T(8,128)} fusion(f32[1,4,16,128,64]{4,3,2,1,0:T(8,128)} %copy.164, f32[4,16,128,64]{3,2,1,0:T(8,128)} %get-tuple-element.426, f32[4,16]{1,0:T(4,128)S(1)} %dynamic-slice_bitcast_fusion.4), kind=kLoop, calls=%fused_computation.clone.1 | loop fusion | flops 1048576 | bytes 6291712 | tf_op jit(solution)/shard_map/while/body/add | solution.py:50
  394.8 2.8 copy.164
  398.2 6.0 %bitcast_add_fusion.10 = f32[4,16,128,64]{3,2,1,0:T(8,128)} fusion(f32[1,4,16,128,64]{4,3,2,1,0:T(8,128)} %copy.164, f32[4,16,128,64]{3,2,1,0:T(8,128)} %get-tuple-element.426, f32[4,16]{1,0:T(4,128)S(1)} %dynamic-slice_bitcast_fusion.4), kind=kLoop, calls=%fused_computation.clone.1 | loop fusion | flops 1048576 | bytes 6291712 | tf_op jit(solution)/shard_map/while/body/add | solution.py:50
  405.9 2.8 copy.164
  409.3 6.0 %bitcast_add_fusion.10 = f32[4,16,128,64]{3,2,1,0:T(8,128)} fusion(f32[1,4,16,128,64]{4,3,2,1,0:T(8,128)} %copy.164, f32[4,16,128,64]{3,2,1,0:T(8,128)} %get-tuple-element.426, f32[4,16]{1,0:T(4,128)S(1)} %dynamic-slice_bitcast_fusion.4), kind=kLoop, calls=%fused_computation.clone.1 | loop fusion | flops 1048576 | bytes 6291712 | tf_op jit(solution)/shard_map/while/body/add | solution.py:50
  417.1 2.8 copy.164
  420.5 6.0 %bitcast_add_fusion.10 = f32[4,16,128,64]{3,2,1,0:T(8,128)} fusion(f32[1,4,16,128,64]{4,3,2,1,0:T(8,128)} %copy.164, f32[4,16,128,64]{3,2,1,0:T(8,128)} %get-tuple-element.426, f32[4,16]{1,0:T(4,128)S(1)} %dynamic-slice_bitcast_fusion.4), kind=kLoop, calls=%fused_computation.clone.1 | loop fusion | flops 1048576 | bytes 6291712 | tf_op jit(solution)/shard_map/while/body/add | solution.py:50
  428.3 2.8 copy.164
  431.7 6.0 %bitcast_add_fusion.10 = f32[4,16,128,64]{3,2,1,0:T(8,128)} fusion(f32[1,4,16,128,64]{4,3,2,1,0:T(8,128)} %copy.164, f32[4,16,128,64]{3,2,1,0:T(8,128)} %get-tuple-element.426, f32[4,16]{1,0:T(4,128)S(1)} %dynamic-slice_bitcast_fusion.4), kind=kLoop, calls=%fused_computation.clone.1 | loop fusion | flops 1048576 | bytes 6291712 | tf_op jit(solution)/shard_map/while/body/add | solution.py:50
  439.4 2.8 copy.164
  442.9 6.0 %bitcast_add_fusion.10 = f32[4,16,128,64]{3,2,1,0:T(8,128)} fusion(f32[1,4,16,128,64]{4,3,2,1,0:T(8,128)} %copy.164, f32[4,16,128,64]{3,2,1,0:T(8,128)} %get-tuple-element.426, f32[4,16]{1,0:T(4,128)S(1)} %dynamic-slice_bitcast_fusion.4), kind=kLoop, calls=%fused_computation.clone.1 | loop fusion | flops 1048576 | bytes 6291712 | tf_op jit(solution)/shard_map/while/body/add | solution.py:50
  450.6 2.8 copy.164
  454.0 6.0 %bitcast_add_fusion.10 = f32[4,16,128,64]{3,2,1,0:T(8,128)} fusion(f32[1,4,16,128,64]{4,3,2,1,0:T(8,128)} %copy.164, f32[4,16,128,64]{3,2,1,0:T(8,128)} %get-tuple-element.426, f32[4,16]{1,0:T(4,128)S(1)} %dynamic-slice_bitcast_fusion.4), kind=kLoop, calls=%fused_computation.clone.1 | loop fusion | flops 1048576 | bytes 6291712 | tf_op jit(solution)/shard_map/while/body/add | solution.py:50
  461.8 2.8 copy.164
  465.2 6.0 %bitcast_add_fusion.10 = f32[4,16,128,64]{3,2,1,0:T(8,128)} fusion(f32[1,4,16,128,64]{4,3,2,1,0:T(8,128)} %copy.164, f32[4,16,128,64]{3,2,1,0:T(8,128)} %get-tuple-element.426, f32[4,16]{1,0:T(4,128)S(1)} %dynamic-slice_bitcast_fusion.4), kind=kLoop, calls=%fused_computation.clone.1 | loop fusion | flops 1048576 | bytes 6291712 | tf_op jit(solution)/shard_map/while/body/add | solution.py:50
  472.9 2.8 copy.164
  476.4 6.0 %bitcast_add_fusion.10 = f32[4,16,128,64]{3,2,1,0:T(8,128)} fusion(f32[1,4,16,128,64]{4,3,2,1,0:T(8,128)} %copy.164, f32[4,16,128,64]{3,2,1,0:T(8,128)} %get-tuple-element.426, f32[4,16]{1,0:T(4,128)S(1)} %dynamic-slice_bitcast_fusion.4), kind=kLoop, calls=%fused_computation.clone.1 | loop fusion | flops 1048576 | bytes 6291712 | tf_op jit(solution)/shard_map/while/body/add | solution.py:50
  484.1 2.8 copy.164
  487.5 6.0 %bitcast_add_fusion.10 = f32[4,16,128,64]{3,2,1,0:T(8,128)} fusion(f32[1,4,16,128,64]{4,3,2,1,0:T(8,128)} %copy.164, f32[4,16,128,64]{3,2,1,0:T(8,128)} %get-tuple-element.426, f32[4,16]{1,0:T(4,128)S(1)} %dynamic-slice_bitcast_fusion.4), kind=kLoop, calls=%fused_computation.clone.1 | loop fusion | flops 1048576 | bytes 6291712 | tf_op jit(solution)/shard_map/while/body/add | solution.py:50
  495.3 2.8 copy.164
  498.7 6.0 %bitcast_add_fusion.10 = f32[4,16,128,64]{3,2,1,0:T(8,128)} fusion(f32[1,4,16,128,64]{4,3,2,1,0:T(8,128)} %copy.164, f32[4,16,128,64]{3,2,1,0:T(8,128)} %get-tuple-element.426, f32[4,16]{1,0:T(4,128)S(1)} %dynamic-slice_bitcast_fusion.4), kind=kLoop, calls=%fused_computation.clone.1 | loop fusion | flops 1048576 | bytes 6291712 | tf_op jit(solution)/shard_map/while/body/add | solution.py:50
  506.4 2.8 copy.164
  509.9 6.0 %bitcast_add_fusion.10 = f32[4,16,128,64]{3,2,1,0:T(8,128)} fusion(f32[1,4,16,128,64]{4,3,2,1,0:T(8,128)} %copy.164, f32[4,16,128,64]{3,2,1,0:T(8,128)} %get-tuple-element.426, f32[4,16]{1,0:T(4,128)S(1)} %dynamic-slice_bitcast_fusion.4), kind=kLoop, calls=%fused_computation.clone.1 | loop fusion | flops 1048576 | bytes 6291712 | tf_op jit(solution)/shard_map/while/body/add | solution.py:50
  521.0 6.0 %bitcast_add_fusion.10 = f32[4,16,128,64]{3,2,1,0:T(8,128)} fusion(f32[1,4,16,128,64]{4,3,2,1,0:T(8,128)} %copy.164, f32[4,16,128,64]{3,2,1,0:T(8,128)} %get-tuple-element.426, f32[4,16]{1,0:T(4,128)S(1)} %dynamic-slice_bitcast_fusion.4), kind=kLoop, calls=%fused_computation.clone.1 | loop fusion | flops 1048576 | bytes 6291712 | tf_op jit(solution)/shard_map/while/body/add | solution.py:50
  532.2 6.0 %bitcast_add_fusion.10 = f32[4,16,128,64]{3,2,1,0:T(8,128)} fusion(f32[1,4,16,128,64]{4,3,2,1,0:T(8,128)} %copy.164, f32[4,16,128,64]{3,2,1,0:T(8,128)} %get-tuple-element.426, f32[4,16]{1,0:T(4,128)S(1)} %dynamic-slice_bitcast_fusion.4), kind=kLoop, calls=%fused_computation.clone.1 | loop fusion | flops 1048576 | bytes 6291712 | tf_op jit(solution)/shard_map/while/body/add | solution.py:50
  538.3 7.7 %multiply_reduce_fusion = (f32[128,4,16]{0,2,1:T(8,128)S(1)}, f32[128,4,16]{0,2,1:T(8,128)}, bf16[1,128,4,16,64]{1,4,3,2,0:T(8,128)(2,1)S(1)}) fusion(f32[1,128,4,16,64]{1,4,3,2,0:T(8,128)} %bitcast.185, f32[128,4,16]{0,2,1:T(8,128)} %bitcast.200, f32[4,16,128,64]{3,2,1,0:T(8,128)} %get-tuple-element.216, bf16[128,4,128,1]{2,1,0,3:T(4,128)(2,1)S(1)} %bitcast.191, ...), kind=kOutput, calls=%fused_computation.31 | convolution fusion | flops 810008576 | bytes 7602176 | tf_op jit(solution)/shard_map/kjgn,kghnp,ghkj->kjghp/dot_general | solution.py:131
  546.1 17.0 %all-gather.1 = f32[16,1,64]{2,1,0:T(1,128)S(1)} all-gather(f32[1,1,64]{2,1,0:T(1,128)S(1)} %reshape.380), channel_id=1, replica_groups=mesh['context'=16,'tensor'=2] {'context'}, dimensions={0}, use_global_device_ids=true | all-gather | bytes 4352 | tf_op jit(solution)/shard_map/all_gather | solution.py:35
  563.9 6.7 %fusion.34 = f32[1,128,4,128]{1,3,2,0:T(8,128)} fusion(f32[1,128,4,128]{1,3,2,0:T(8,128)S(1)} %copy-done.6, f32[4,16,128,64]{3,2,1,0:T(8,128)} %get-tuple-element.216, f32[128,4,16,64]{0,3,2,1:T(8,128)S(1)} %bitcast.186, f32[4,16,128]{2,1,0:T(8,128)} %get-tuple-element.313, f32[128,4,16]{0,2,1:T(8,128)} %bitcast.201), kind=kOutput, calls=%fused_computation.53 | convolution fusion | flops 806420480 | bytes 4784128 | tf_op jit(solution)/shard_map/kjghp,kghnp,ghkj->kjgn/dot_general | solution.py:135
  (148 shorter events, 83.7 us)
Async XLA Ops:
  7.2 190.9 %all-gather.7.cloned.1.call-start = ((), (), s32[]{:S(2)}) async-start(), calls=%async_computation.2 | async-start | bytes 35651584 | tf_op jit(solution)/shard_map/all_gather | solution.py:35
  8.5 10.2 %collective-permute-start.1 = (s32[1]{0:T(128)}, s32[1]{0:T(128)}, u32[]{:S(2)}, u32[]{:S(2)}) collective-permute-start(s32[1]{0:T(128)} %get-tuple-element.319), channel_id=1, source_target_pairs={{0,2},{2,4},{4,6},{6,8},{8,10},{10,12},{12,14},{14,16},{16,18},{18... | collective-permute-start | bytes 20 | tf_op jit(solution)/shard_map/ppermute | solution.py:22
  11.4 9.2 %collective-permute-start = (s32[1]{0:T(128)}, s32[1]{0:T(128)}, u32[]{:S(2)}, u32[]{:S(2)}) collective-permute-start(s32[1]{0:T(128)} %get-tuple-element.318), channel_id=1, source_target_pairs={{2,0},{4,2},{6,4},{8,6},{10,8},{12,10},{14,12},{16,14},{18,16},{20... | collective-permute-start | bytes 20 | tf_op jit(solution)/shard_map/ppermute | solution.py:24
  16.6 5.3 copy-start.10
  16.8 1.8 copy-start.15
  18.5 2.8 copy-start.19
  18.5 4.1 copy-start.7
  18.6 118.0 %copy-start = (f32[128,4096]{0,1:T(8,128)}, f32[128,4096]{0,1:T(8,128)S(1)}, u32[]{:S(2)}) copy-start(f32[128,4096]{0,1:T(8,128)S(1)} %convert_element_type.47) | copy-start | bytes 6291460
  21.9 3.3 copy-start.17
  21.9 3.3 copy-start.21
  22.6 29.6 %copy-start.8 = (f32[4,16,128]{2,1,0:T(8,128)}, f32[4,16,128]{2,1,0:T(8,128)S(1)}, u32[]{:S(2)}) copy-start(f32[4,16,128]{2,1,0:T(8,128)S(1)} %get-tuple-element.314) | copy-start | bytes 98308
  25.2 1.2 copy-start.5
  27.4 17.5 %all-to-all-start = ((bf16[64,2,4096]{2,0,1:T(8,128)(2,1)}), bf16[64,2,4096]{2,0,1:T(8,128)(2,1)S(1)}, u32[]{:S(2)}, u32[]{:S(2)}) async-start(bf16[64,2,4096]{2,0,1:T(8,128)(2,1)} %bitcast.189), calls=%async_computation | async-start | bytes 2097152 | tf_op jit(solution)/shard_map/all_to_all | solution.py:60
  31.1 337.1 %all-gather.5.cloned.1.call-start = ((), (), s32[]{:S(2)}) async-start(), calls=%async_computation.1 | async-start | bytes 35651584 | tf_op jit(solution)/shard_map/all_gather | solution.py:35
  56.0 1.6 copy-start.25
  60.2 6.9 %copy-start.12 = (f32[4,128,128]{1,2,0:T(8,128)}, f32[4,128,128]{1,2,0:T(8,128)S(1)}, u32[]{:S(2)}) copy-start(f32[4,128,128]{1,2,0:T(8,128)S(1)} %fusion.62) | copy-start | bytes 786436
  131.8 4.9 copy-start.2
  136.7 5.7 copy-start.4
  136.7 7.8 %copy-start.11 = (f32[4,16,1,128]{3,1,2,0:T(8,128)S(1)}, f32[4,16,1,128]{3,1,2,0:T(8,128)}, u32[]{:S(2)}) copy-start(f32[4,16,1,128]{3,1,2,0:T(8,128)} %copy-done.10) | copy-start | bytes 98308
  136.7 7.8 %copy-start.13 = (f32[4,128,128]{1,2,0:T(8,128)S(1)}, f32[4,128,128]{1,2,0:T(8,128)}, u32[]{:S(2)}) copy-start(f32[4,128,128]{1,2,0:T(8,128)} %copy-done.12) | copy-start | bytes 786436
  200.6 0.8 copy-start.9
  201.3 8.6 %copy-start.3 = (f32[1,128,4,16,64]{1,4,3,2,0:T(8,128)S(1)}, f32[1,128,4,16,64]{1,4,3,2,0:T(8,128)}, u32[]{:S(2)}) copy-start(f32[1,128,4,16,64]{1,4,3,2,0:T(8,128)} %copy.112) | copy-start | bytes 6291460
  538.2 7.7 %copy-start.14 = (f32[128,4,16]{0,2,1:T(8,128)S(1)}, f32[128,4,16]{0,2,1:T(8,128)}, u32[]{:S(2)}) copy-start(f32[128,4,16]{0,2,1:T(8,128)} %fusion.11) | copy-start | bytes 98308
  538.2 7.7 %copy-start.18 = (f32[128]{0:T(128)S(1)}, f32[128]{0:T(128)}, u32[]{:S(2)}) copy-start(f32[128]{0:T(128)} %copy-done.17) | copy-start | bytes 1540
  538.2 24.9 %copy-start.23 = (f32[16]{0:T(128)S(1)}, f32[16]{0:T(128)}, u32[]{:S(2)}) copy-start(f32[16]{0:T(128)} %all-reduce) | copy-start | bytes 196
  538.2 25.6 %copy-start.1 = (f32[128,4096]{0,1:T(8,128)S(1)}, f32[128,4096]{0,1:T(8,128)}, u32[]{:S(2)}) copy-start(f32[128,4096]{0,1:T(8,128)} %copy-done) | copy-start | bytes 6291460
  538.2 25.6 %copy-start.6 = (f32[1,128,4,128]{1,3,2,0:T(8,128)S(1)}, f32[1,128,4,128]{1,3,2,0:T(8,128)}, u32[]{:S(2)}) copy-start(f32[1,128,4,128]{1,3,2,0:T(8,128)} %convolution_bitcast_fusion.1) | copy-start | bytes 786436
  570.6 3.1 copy-start.16
  570.6 3.1 copy-start.20
  570.6 3.1 copy-start.22
  570.6 3.1 copy-start.24
Sparse Core Ops, SparseCore 0:
  25.3 172.7 all-gather.6
  199.7 168.4 all-gather.4
where the time goes:
time: 583 us; the launch traced here: 581 us
  waiting for transfers between devices  212 us (36%)
  local copies, waits for them, and re-layouts  117 us (20%)
  other arithmetic  98.1 us (17%)
  blocking collectives  72.3 us (12%)
  matrix products  57.4 us (10%)
  between operations  16.9 us (3%)
  starting transfers between devices  7.87 us (1%)
    all_gather x2, waiting for transfers between devices, entering(): gathered = jax.tree.map(lambda a: lax.all_gather(a, axis), part)  199 us
    add x30, other arithmetic, link_pairs(): return (earlier[0] * decay_late, spread * earlier[1] + later[1])  90.3 us
    dynamic_slice x30, local copies, waits for them, and re-layouts, one(): lax.dynamic_index_in_dim(a, source, 0, False)  67.3 us
    all_gather x2, blocking collectives, entering(): gathered = jax.tree.map(lambda a: lax.all_gather(a, axis), part)  36.4 us
    unnamed x1, blocking collectives  35.9 us
    another operation x8, local copies, waits for them, and re-layouts  14.3 us
    all_to_all x1, waiting for transfers between devices, shards(): lax.all_to_all(grad_output, 'tensor', split_axis=1, concat_axis=0, tiled=...  12.9 us
    unnamed x62, local copies, waits for them, and re-layouts  12.1 us
  transfers between devices with their start and end apart: 5, of which 3 were waited for; matrix products, arithmetic and copies ran while one was open for 13% of the time, Pallas kernels for 0%

commit v1 on v0

--- a/solution.py
+++ b/solution.py
@@ -57,7 +57,12 @@
     groups_here = heads_here // per_group
     span = min(BLOCK, tokens_here)
     count = tokens_here // span
-    local_grads = lax.all_to_all(grad_output, "tensor", split_axis=1, concat_axis=0, tiled=True)
+    local_grads = jnp.concatenate(
+        lax.all_to_all(
+            jnp.stack(jnp.split(grad_output, lax.axis_size("tensor"), axis=1)), "tensor", 0, 0
+        ),
+        axis=0,
+    )
     shifted_ids = document + 1
     rim = padded(shifted_ids, (("context", 0),), 1)
     prev_id = rim[0] - 1

time: 583 us -> 584 us (level)
    another operation x8 -> x9, local copies, waits for them, and re-layouts: 14.3 us -> 16.5 us
    unnamed x62 -> x58, local copies, waits for them, and re-layouts: 12.1 us -> 10.8 us
where the time goes in v1:
time: 584 us; the launch traced here: 582 us
  waiting for transfers between devices  214 us (37%)
  local copies, waits for them, and re-layouts  115 us (20%)
  other arithmetic  97.7 us (17%)
  blocking collectives  72.4 us (12%)
  matrix products  57.8 us (10%)
  between operations  16.9 us (3%)
  starting transfers between devices  7.99 us (1%)
    all_gather x2, waiting for transfers between devices, entering(): gathered = jax.tree.map(lambda a: lax.all_gather(a, axis), part)  201 us
    add x30, other arithmetic, link_pairs(): return (earlier[0] * decay_late, spread * earlier[1] + later[1])  90.4 us
    dynamic_slice x30, local copies, waits for them, and re-layouts, one(): lax.dynamic_index_in_dim(a, source, 0, False)  67.4 us
    all_gather x2, blocking collectives, entering(): gathered = jax.tree.map(lambda a: lax.all_gather(a, axis), part)  36.5 us
    unnamed x1, blocking collectives  36 us
    another operation x8, local copies, waits for them, and re-layouts  15.2 us
    all_to_all x1, waiting for transfers between devices, shards(): lax.all_to_all(jnp.stack(jnp.split(grad_output, lax.axis_size('tensor'),...  12.6 us
  transfers between devices with their start and end apart: 5, of which 3 were waited for; matrix products, arithmetic and copies ran while one was open for 13% of the time, Pallas kernels for 0%

profile of v1, /device:TPU:0, one launch (start us, length us, event | category | flops | bytes accessed | tf_op | source)
XLA Modules:
  0.0 582.5 jit_solution(16932664185258380720)
XLA Ops:
  8.5 2.9 collective-permute-start.1
  28.3 3.6 all-to-all-start
  33.1 12.6 %all-to-all-done = bf16[2,64,4096]{2,1,0:T(8,128)(2,1)S(1)} async-done(((bf16[2,64,4096]{2,1,0:T(8,128)(2,1)}), bf16[2,64,4096]{2,1,0:T(8,128)(2,1)S(1)}, u32[]{:S(2)}, u32[]{:S(2)}) %all-to-all-start) | async-done | bytes 1048608 | tf_op jit(solution)/shard_map/all_to_all | solution.py:61
  45.7 3.3 reshape.359
  49.0 4.0 copy.83
  53.0 3.8 fusion.13
  61.0 10.5 %fusion.1 = f32[4,16,64,128]{3,2,1,0:T(8,128)} fusion(f32[4,128,128]{2,1,0:T(8,128)S(1)} %fusion.61, f32[4,16,128]{2,1,0:T(8,128)} %bitcast.195, pred[128,128]{1,0:T(8,128)(4,1)S(1)} %fusion.54, f32[128,4,16,64]{0,3,2,1:T(8,128)S(1)} %bitcast.175, f32[128,4,16]{0,2,1:T(8,128)} %bitcast.187), kind=kOutput, calls=%fused_computation.11 | convolution fusion | flops 810024960 | bytes 4538368 | tf_op jit(solution)/shard_map/ghkij,kjghp->kighp/dot_general | solution.py:143
  74.7 36.0 %all-reduce = f32[16]{0:T(128)} all-reduce(f32[16]{0:T(128)} %dynamic-update-slice), channel_id=2, replica_groups=mesh['context'=16,'tensor'=2] {'context'}, use_global_device_ids=true, to_apply=%add | all-reduce | flops 16 | bytes 128
  110.7 19.4 %all-gather = f32[64,16,1,1]{1,3,2,0:T(1,128)} all-gather(f32[4,16,1,1]{1,3,2,0:T(1,128)} %bitcast.203), channel_id=3, replica_groups=mesh['context'=16,'tensor'=2] {'context'}, dimensions={0}, use_global_device_ids=true | all-gather | bytes 4352 | tf_op jit(solution)/shard_map/all_gather | solution.py:35
  130.2 3.2 reshape.371
  133.4 4.9 copy.96
  138.3 4.3 multiply_reduce_fusion
  144.7 4.4 fusion.3
  149.1 49.8 %all-gather.7.cloned.1.call-done = f32[16,4,16,128,64]{3,4,2,1,0:T(8,128)} async-done(((f32[1,4,16,128,64]{3,4,2,1,0:T(8,128)}), f32[16,4,16,128,64]{3,4,2,1,0:T(8,128)}) %all-gather.7.cloned.1.call-update) | async-done | bytes 33554448 | tf_op jit(solution)/shard_map/all_gather | solution.py:35
  202.2 6.8 %fusion.37 = f32[1,128,4,128]{1,3,2,0:T(8,128)} fusion(f32[1,128,4,128]{1,3,2,0:T(8,128)} %convolution_bitcast_fusion, f32[4,16,128,64]{3,2,1,0:T(8,128)} %get-tuple-element.217, bf16[128,4,16,64]{0,3,2,1:T(8,128)(2,1)S(1)} %copy-done.2, f32[4,16,128]{2,1,0:T(8,128)S(1)} %copy-done.8), kind=kOutput, calls=%fused_computation.54 | convolution fusion | flops 806420480 | bytes 3702784 | tf_op jit(solution)/shard_map/kighp,kghnp,ghki->kign/dot_general | solution.py:139
  210.8 6.9 %fusion.10 = f32[128,4,16]{0,2,1:T(8,128)} fusion(f32[1,128,4,16,64]{1,4,3,2,0:T(8,128)S(1)} %copy-done.3, f32[4,16,64,128]{3,2,1,0:T(8,128)} %fusion.1, f32[4,16,128,64]{3,2,1,0:T(8,128)} %get-tuple-element.217, f32[128,4,16]{0,2,1:T(8,128)S(1)} %bitcast.193, bf16[128,4,128,1]{2,1,0,3:T(4,128)(2,1)S(1)} %bitcast.183), kind=kOutput, calls=%fused_computation.20 | convolution fusion | flops 807395328 | bytes 6488064 | tf_op jit(solution)/shard_map/kign,kghnp,ghki->kighp/dot_general | solution.py:135
  217.8 151.2 %all-gather.5.cloned.1.call-done = f32[16,4,16,128,64]{3,4,2,1,0:T(8,128)} async-done(((f32[1,4,16,128,64]{3,4,2,1,0:T(8,128)}), f32[16,4,16,128,64]{3,4,2,1,0:T(8,128)}) %all-gather.5.cloned.1.call-update) | async-done | bytes 33554448 | tf_op jit(solution)/shard_map/all_gather | solution.py:35
  371.6 167.7 %while.40 = (s32[]{:T(128)}, f32[4,16,128,64]{3,2,1,0:T(8,128)}, s32[]{:T(128)}, f32[16,4,16]{2,1,0:T(4,128)}, f32[16,4,16,128,64]{3,4,2,1,0:T(8,128)}, /*index=5*/s32[]{:T(128)}, s32[]{:T(128)}, s32[]{:T(128)}, s32[]{:T(128)}) while((s32[]{:T(128)}, f32[4,16,128,64]{3,2,1,0:T(8,128)}, s32[]{:T(128)}, f32[16,4,16]{2,1,0:T(4,128)}, ...), condition=%wide.region_2.3_spmd, body=%wide.region_1.2_spmd.sunk | while | flops 1048582 | bytes 14680979 | solution.py:44
  373.3 2.8 copy.138
  376.7 6.0 %bitcast_add_fusion.10 = f32[4,16,128,64]{3,2,1,0:T(8,128)} fusion(f32[1,4,16,128,64]{4,3,2,1,0:T(8,128)} %copy.138, f32[4,16,128,64]{3,2,1,0:T(8,128)} %get-tuple-element.428, f32[4,16]{1,0:T(4,128)S(1)} %dynamic-slice_bitcast_fusion.4), kind=kLoop, calls=%fused_computation.clone.1 | loop fusion | flops 1048576 | bytes 6291712 | tf_op jit(solution)/shard_map/while/body/add | solution.py:50
  384.5 2.8 copy.138
  387.9 6.0 %bitcast_add_fusion.10 = f32[4,16,128,64]{3,2,1,0:T(8,128)} fusion(f32[1,4,16,128,64]{4,3,2,1,0:T(8,128)} %copy.138, f32[4,16,128,64]{3,2,1,0:T(8,128)} %get-tuple-element.428, f32[4,16]{1,0:T(4,128)S(1)} %dynamic-slice_bitcast_fusion.4), kind=kLoop, calls=%fused_computation.clone.1 | loop fusion | flops 1048576 | bytes 6291712 | tf_op jit(solution)/shard_map/while/body/add | solution.py:50
  395.7 2.8 copy.138
  399.1 6.0 %bitcast_add_fusion.10 = f32[4,16,128,64]{3,2,1,0:T(8,128)} fusion(f32[1,4,16,128,64]{4,3,2,1,0:T(8,128)} %copy.138, f32[4,16,128,64]{3,2,1,0:T(8,128)} %get-tuple-element.428, f32[4,16]{1,0:T(4,128)S(1)} %dynamic-slice_bitcast_fusion.4), kind=kLoop, calls=%fused_computation.clone.1 | loop fusion | flops 1048576 | bytes 6291712 | tf_op jit(solution)/shard_map/while/body/add | solution.py:50
  406.8 2.8 copy.138
  410.3 6.0 %bitcast_add_fusion.10 = f32[4,16,128,64]{3,2,1,0:T(8,128)} fusion(f32[1,4,16,128,64]{4,3,2,1,0:T(8,128)} %copy.138, f32[4,16,128,64]{3,2,1,0:T(8,128)} %get-tuple-element.428, f32[4,16]{1,0:T(4,128)S(1)} %dynamic-slice_bitcast_fusion.4), kind=kLoop, calls=%fused_computation.clone.1 | loop fusion | flops 1048576 | bytes 6291712 | tf_op jit(solution)/shard_map/while/body/add | solution.py:50
  418.0 2.8 copy.138
  421.5 6.0 %bitcast_add_fusion.10 = f32[4,16,128,64]{3,2,1,0:T(8,128)} fusion(f32[1,4,16,128,64]{4,3,2,1,0:T(8,128)} %copy.138, f32[4,16,128,64]{3,2,1,0:T(8,128)} %get-tuple-element.428, f32[4,16]{1,0:T(4,128)S(1)} %dynamic-slice_bitcast_fusion.4), kind=kLoop, calls=%fused_computation.clone.1 | loop fusion | flops 1048576 | bytes 6291712 | tf_op jit(solution)/shard_map/while/body/add | solution.py:50
  429.2 2.8 copy.138
  432.6 6.0 %bitcast_add_fusion.10 = f32[4,16,128,64]{3,2,1,0:T(8,128)} fusion(f32[1,4,16,128,64]{4,3,2,1,0:T(8,128)} %copy.138, f32[4,16,128,64]{3,2,1,0:T(8,128)} %get-tuple-element.428, f32[4,16]{1,0:T(4,128)S(1)} %dynamic-slice_bitcast_fusion.4), kind=kLoop, calls=%fused_computation.clone.1 | loop fusion | flops 1048576 | bytes 6291712 | tf_op jit(solution)/shard_map/while/body/add | solution.py:50
  440.4 2.8 copy.138
  443.8 6.0 %bitcast_add_fusion.10 = f32[4,16,128,64]{3,2,1,0:T(8,128)} fusion(f32[1,4,16,128,64]{4,3,2,1,0:T(8,128)} %copy.138, f32[4,16,128,64]{3,2,1,0:T(8,128)} %get-tuple-element.428, f32[4,16]{1,0:T(4,128)S(1)} %dynamic-slice_bitcast_fusion.4), kind=kLoop, calls=%fused_computation.clone.1 | loop fusion | flops 1048576 | bytes 6291712 | tf_op jit(solution)/shard_map/while/body/add | solution.py:50
  451.6 2.8 copy.138
  455.0 6.0 %bitcast_add_fusion.10 = f32[4,16,128,64]{3,2,1,0:T(8,128)} fusion(f32[1,4,16,128,64]{4,3,2,1,0:T(8,128)} %copy.138, f32[4,16,128,64]{3,2,1,0:T(8,128)} %get-tuple-element.428, f32[4,16]{1,0:T(4,128)S(1)} %dynamic-slice_bitcast_fusion.4), kind=kLoop, calls=%fused_computation.clone.1 | loop fusion | flops 1048576 | bytes 6291712 | tf_op jit(solution)/shard_map/while/body/add | solution.py:50
  462.7 2.8 copy.138
  466.2 6.0 %bitcast_add_fusion.10 = f32[4,16,128,64]{3,2,1,0:T(8,128)} fusion(f32[1,4,16,128,64]{4,3,2,1,0:T(8,128)} %copy.138, f32[4,16,128,64]{3,2,1,0:T(8,128)} %get-tuple-element.428, f32[4,16]{1,0:T(4,128)S(1)} %dynamic-slice_bitcast_fusion.4), kind=kLoop, calls=%fused_computation.clone.1 | loop fusion | flops 1048576 | bytes 6291712 | tf_op jit(solution)/shard_map/while/body/add | solution.py:50
  473.9 2.8 copy.138
  477.4 6.0 %bitcast_add_fusion.10 = f32[4,16,128,64]{3,2,1,0:T(8,128)} fusion(f32[1,4,16,128,64]{4,3,2,1,0:T(8,128)} %copy.138, f32[4,16,128,64]{3,2,1,0:T(8,128)} %get-tuple-element.428, f32[4,16]{1,0:T(4,128)S(1)} %dynamic-slice_bitcast_fusion.4), kind=kLoop, calls=%fused_computation.clone.1 | loop fusion | flops 1048576 | bytes 6291712 | tf_op jit(solution)/shard_map/while/body/add | solution.py:50
  488.5 6.0 %bitcast_add_fusion.10 = f32[4,16,128,64]{3,2,1,0:T(8,128)} fusion(f32[1,4,16,128,64]{4,3,2,1,0:T(8,128)} %copy.138, f32[4,16,128,64]{3,2,1,0:T(8,128)} %get-tuple-element.428, f32[4,16]{1,0:T(4,128)S(1)} %dynamic-slice_bitcast_fusion.4), kind=kLoop, calls=%fused_computation.clone.1 | loop fusion | flops 1048576 | bytes 6291712 | tf_op jit(solution)/shard_map/while/body/add | solution.py:50
  499.7 6.0 %bitcast_add_fusion.10 = f32[4,16,128,64]{3,2,1,0:T(8,128)} fusion(f32[1,4,16,128,64]{4,3,2,1,0:T(8,128)} %copy.138, f32[4,16,128,64]{3,2,1,0:T(8,128)} %get-tuple-element.428, f32[4,16]{1,0:T(4,128)S(1)} %dynamic-slice_bitcast_fusion.4), kind=kLoop, calls=%fused_computation.clone.1 | loop fusion | flops 1048576 | bytes 6291712 | tf_op jit(solution)/shard_map/while/body/add | solution.py:50
  507.4 2.8 copy.138
  510.9 6.0 %bitcast_add_fusion.10 = f32[4,16,128,64]{3,2,1,0:T(8,128)} fusion(f32[1,4,16,128,64]{4,3,2,1,0:T(8,128)} %copy.138, f32[4,16,128,64]{3,2,1,0:T(8,128)} %get-tuple-element.428, f32[4,16]{1,0:T(4,128)S(1)} %dynamic-slice_bitcast_fusion.4), kind=kLoop, calls=%fused_computation.clone.1 | loop fusion | flops 1048576 | bytes 6291712 | tf_op jit(solution)/shard_map/while/body/add | solution.py:50
  518.6 2.8 copy.138
  522.1 6.0 %bitcast_add_fusion.10 = f32[4,16,128,64]{3,2,1,0:T(8,128)} fusion(f32[1,4,16,128,64]{4,3,2,1,0:T(8,128)} %copy.138, f32[4,16,128,64]{3,2,1,0:T(8,128)} %get-tuple-element.428, f32[4,16]{1,0:T(4,128)S(1)} %dynamic-slice_bitcast_fusion.4), kind=kLoop, calls=%fused_computation.clone.1 | loop fusion | flops 1048576 | bytes 6291712 | tf_op jit(solution)/shard_map/while/body/add | solution.py:50
  533.2 6.0 %bitcast_add_fusion.10 = f32[4,16,128,64]{3,2,1,0:T(8,128)} fusion(f32[1,4,16,128,64]{4,3,2,1,0:T(8,128)} %copy.138, f32[4,16,128,64]{3,2,1,0:T(8,128)} %get-tuple-element.428, f32[4,16]{1,0:T(4,128)S(1)} %dynamic-slice_bitcast_fusion.4), kind=kLoop, calls=%fused_computation.clone.1 | loop fusion | flops 1048576 | bytes 6291712 | tf_op jit(solution)/shard_map/while/body/add | solution.py:50
  539.3 7.7 %multiply_reduce_fusion.1 = (f32[128,4,16]{0,2,1:T(8,128)S(1)}, f32[128,4,16]{0,2,1:T(8,128)}, bf16[1,128,4,16,64]{1,4,3,2,0:T(8,128)(2,1)S(1)}) fusion(f32[1,128,4,16,64]{1,4,3,2,0:T(8,128)} %bitcast.177, f32[128,4,16]{0,2,1:T(8,128)} %bitcast.189, f32[4,16,128,64]{3,2,1,0:T(8,128)} %get-tuple-element.216, bf16[128,4,128,1]{2,1,0,3:T(4,128)(2,1)S(1)} %bitcast.181, ...), kind=kOutput, calls=%fused_computation.30 | convolution fusion | flops 810008576 | bytes 7602176 | tf_op jit(solution)/shard_map/kjgn,kghnp,ghkj->kjghp/dot_general | solution.py:136
  547.1 17.0 %all-gather.1 = f32[16,1,64]{2,1,0:T(1,128)S(1)} all-gather(f32[1,1,64]{2,1,0:T(1,128)S(1)} %reshape.378), channel_id=1, replica_groups=mesh['context'=16,'tensor'=2] {'context'}, dimensions={0}, use_global_device_ids=true | all-gather | bytes 4352 | tf_op jit(solution)/shard_map/all_gather | solution.py:35
  564.9 6.7 %fusion.33 = f32[1,128,4,128]{1,3,2,0:T(8,128)} fusion(f32[1,128,4,128]{1,3,2,0:T(8,128)S(1)} %copy-done.5, f32[4,16,128,64]{3,2,1,0:T(8,128)} %get-tuple-element.216, f32[128,4,16,64]{0,3,2,1:T(8,128)S(1)} %bitcast.178, f32[4,16,128]{2,1,0:T(8,128)} %get-tuple-element.315, f32[128,4,16]{0,2,1:T(8,128)} %bitcast.190), kind=kOutput, calls=%fused_computation.52 | convolution fusion | flops 806420480 | bytes 4784128 | tf_op jit(solution)/shard_map/kjghp,kghnp,ghkj->kjgn/dot_general | solution.py:140
  (144 shorter events, 83.3 us)
Async XLA Ops:
  7.2 191.8 %all-gather.7.cloned.1.call-start = ((), (), s32[]{:S(2)}) async-start(), calls=%async_computation.2 | async-start | bytes 35651584 | tf_op jit(solution)/shard_map/all_gather | solution.py:35
  8.5 11.0 %collective-permute-start.1 = (s32[1]{0:T(128)}, s32[1]{0:T(128)}, u32[]{:S(2)}, u32[]{:S(2)}) collective-permute-start(s32[1]{0:T(128)} %get-tuple-element.321), channel_id=1, source_target_pairs={{0,2},{2,4},{4,6},{6,8},{8,10},{10,12},{12,14},{14,16},{16,18},{18... | collective-permute-start | bytes 20 | tf_op jit(solution)/shard_map/ppermute | solution.py:22
  11.3 10.0 %collective-permute-start = (s32[1]{0:T(128)}, s32[1]{0:T(128)}, u32[]{:S(2)}, u32[]{:S(2)}) collective-permute-start(s32[1]{0:T(128)} %get-tuple-element.320), channel_id=1, source_target_pairs={{2,0},{4,2},{6,4},{8,6},{10,8},{12,10},{14,12},{16,14},{18,16},{20... | collective-permute-start | bytes 20 | tf_op jit(solution)/shard_map/ppermute | solution.py:24
  16.5 6.1 %copy-start.9 = (f32[4,16,1,128]{3,1,2,0:T(8,128)}, f32[4,16,1,128]{3,1,2,0:T(8,128)S(1)}, u32[]{:S(2)}) copy-start(f32[4,16,1,128]{3,1,2,0:T(8,128)S(1)} %reduce_window_sum.11) | copy-start | bytes 98308
  19.3 2.7 copy-start.17
  19.3 4.1 copy-start.6
  19.5 118.8 %copy-start = (f32[128,4096]{0,1:T(8,128)}, f32[128,4096]{0,1:T(8,128)S(1)}, u32[]{:S(2)}) copy-start(f32[128,4096]{0,1:T(8,128)S(1)} %convert_element_type.47) | copy-start | bytes 6291460
  22.7 3.3 copy-start.15
  22.7 3.3 copy-start.19
  23.4 29.6 %copy-start.7 = (f32[4,16,128]{2,1,0:T(8,128)}, f32[4,16,128]{2,1,0:T(8,128)S(1)}, u32[]{:S(2)}) copy-start(f32[4,16,128]{2,1,0:T(8,128)S(1)} %get-tuple-element.316) | copy-start | bytes 98308
  28.3 17.4 %all-to-all-start = ((bf16[2,64,4096]{2,1,0:T(8,128)(2,1)}), bf16[2,64,4096]{2,1,0:T(8,128)(2,1)S(1)}, u32[]{:S(2)}, u32[]{:S(2)}) async-start(bf16[2,64,4096]{2,1,0:T(8,128)(2,1)} %pad_maximum_fusion), calls=%async_computation | async-start | bytes 2097152 | tf_op jit(solution)/shard_map/all_to_all | solution.py:61
  31.9 337.1 %all-gather.5.cloned.1.call-start = ((), (), s32[]{:S(2)}) async-start(), calls=%async_computation.1 | async-start | bytes 35651584 | tf_op jit(solution)/shard_map/all_gather | solution.py:35
  56.8 1.6 copy-start.23
  61.0 10.5 %copy-start.11 = (f32[4,128,128]{2,1,0:T(8,128)}, f32[4,128,128]{2,1,0:T(8,128)S(1)}, u32[]{:S(2)}) copy-start(f32[4,128,128]{2,1,0:T(8,128)S(1)} %fusion.61) | copy-start | bytes 786436
  133.4 4.9 copy-start.2
  138.2 4.4 copy-start.4
  138.2 6.5 %copy-start.10 = (f32[4,16,1,128]{3,1,2,0:T(8,128)S(1)}, f32[4,16,1,128]{3,1,2,0:T(8,128)}, u32[]{:S(2)}) copy-start(f32[4,16,1,128]{3,1,2,0:T(8,128)} %copy-done.9) | copy-start | bytes 98308
  138.3 6.5 %copy-start.12 = (f32[4,128,128]{2,1,0:T(8,128)S(1)}, f32[4,128,128]{2,1,0:T(8,128)}, u32[]{:S(2)}) copy-start(f32[4,128,128]{2,1,0:T(8,128)} %copy-done.11) | copy-start | bytes 786436
  201.4 0.8 copy-start.8
  202.2 8.7 %copy-start.3 = (f32[1,128,4,16,64]{1,4,3,2,0:T(8,128)S(1)}, f32[1,128,4,16,64]{1,4,3,2,0:T(8,128)}, u32[]{:S(2)}) copy-start(f32[1,128,4,16,64]{1,4,3,2,0:T(8,128)} %copy.96) | copy-start | bytes 6291460
  539.2 7.7 %copy-start.13 = (f32[128,4,16]{0,2,1:T(8,128)S(1)}, f32[128,4,16]{0,2,1:T(8,128)}, u32[]{:S(2)}) copy-start(f32[128,4,16]{0,2,1:T(8,128)} %fusion.10) | copy-start | bytes 98308
  539.2 7.7 %copy-start.16 = (f32[128]{0:T(128)S(1)}, f32[128]{0:T(128)}, u32[]{:S(2)}) copy-start(f32[128]{0:T(128)} %copy-done.15) | copy-start | bytes 1540
  539.3 24.9 %copy-start.21 = (f32[16]{0:T(128)S(1)}, f32[16]{0:T(128)}, u32[]{:S(2)}) copy-start(f32[16]{0:T(128)} %all-reduce) | copy-start | bytes 196
  539.3 25.6 %copy-start.1 = (f32[128,4096]{0,1:T(8,128)S(1)}, f32[128,4096]{0,1:T(8,128)}, u32[]{:S(2)}) copy-start(f32[128,4096]{0,1:T(8,128)} %copy-done) | copy-start | bytes 6291460
  539.3 25.6 %copy-start.5 = (f32[1,128,4,128]{1,3,2,0:T(8,128)S(1)}, f32[1,128,4,128]{1,3,2,0:T(8,128)}, u32[]{:S(2)}) copy-start(f32[1,128,4,128]{1,3,2,0:T(8,128)} %convolution_bitcast_fusion.1) | copy-start | bytes 786436
  571.6 3.1 copy-start.14
  571.6 3.1 copy-start.18
  571.6 3.1 copy-start.20
  571.6 3.1 copy-start.22
Sparse Core Ops, SparseCore 0:
  26.1 172.7 all-gather.6
  200.5 168.4 all-gather.4
